TPU v7x, 32 devices: a whole 2x2x4 slice. The times are simulated.
32 devices in a mesh: tp: 4 (over y, x), grp: 8 (over z, core).
Axes of the slice: x: 2, y: 2, z: 4, core: 2. Of those that a mesh axis runs over, the one named last changes fastest.
Arguments:
- low_feats: bfloat16 [384, 16384], P('grp', 'tp'), may hold values from -40 to 40
- mid_feats: bfloat16 [384, 16384], P('grp', 'tp'), may hold values from -40 to 40
- high_feats: bfloat16 [384, 16384], P('grp', 'tp'), may hold values from -40 to 40
- w_low: bfloat16 [16384, 16384], P('tp', 'grp'), may hold values from -3 to 3
- w_mid: bfloat16 [16384, 16384], P('tp', 'grp'), may hold values from -3 to 3
- w_high: bfloat16 [16384, 16384], P('tp', 'grp'), may hold values from -3 to 3
- norm_gain: float32 [16384], P('grp'), may hold values from 0.1 to 1.9
- accepted: int32 [64], replicated, may hold values from 0 to 5, as said below
- assignment: int32 [64], replicated, may hold values from 0 to 63, each once
Outputs:
- drafted: bfloat16 [384, 16384], P('tp', 'grp')
Inputs may be any that keep to these rules, and one draw needn't show every extreme that they name: For every group of 8 consecutive rows starting at a multiple of 8, the sum of accepted + 1 is at most 32, and some group reaches 32; rows 2i and 2i+1 together have at most 8 positions with p <= accepted. `assignment`: each row appears once.
All inputs are finite; a program needn't handle non-finite values.
Results may differ from a plain program's by a relative error of at most 0.0008.
Values may be sent and summed in bfloat16 or wider, within the bound.
A program may use at most 128 MiB of HBM per device.

v0:
```python
import jax
import jax.numpy as jnp
from jax import lax
from jax.sharding import PartitionSpec as P

D = 16384
ROWS_G = 8
POS = 6


EPSILON = 1e-05


def project(features, weights):
    total = jnp.dot(features[0], weights[0], preferred_element_type=jnp.float32)
    total = total + jnp.dot(features[1], weights[1], preferred_element_type=jnp.float32)
    return total + jnp.dot(features[2], weights[2], preferred_element_type=jnp.float32)


def per_device(
    low_feats, mid_feats, high_feats, w_low, w_mid, w_high, norm_gain, accepted, assignment
):
    weights = (w_low, w_mid, w_high)
    group_tokens = low_feats.shape[0]
    all_rows = accepted.shape[0]
    total_tokens = all_rows * POS
    groups = all_rows // ROWS_G
    step_index = jnp.arange(POS, dtype=jnp.int32)
    live_mask = (step_index[None, :] <= accepted[:, None]).astype(jnp.int32)
    source_rows = (assignment[:, None] * POS + step_index[None, :]).reshape(total_tokens)
    capacity = 4 * ROWS_G
    group_live = live_mask.reshape(groups, group_tokens)
    slots = jnp.cumsum(group_live, axis=1) - group_live
    packed_index = (jnp.arange(groups, dtype=jnp.int32)[:, None] * capacity + slots).reshape(
        total_tokens
    )
    own_group = lax.dynamic_index_in_dim(group_live, lax.axis_index("grp"), 0, keepdims=False)
    ranking = jnp.argsort(1 - own_group, stable=True)[:capacity]
    partial_value = project(
        (
            lax.all_gather(low_feats[ranking], "grp", axis=0, tiled=True),
            lax.all_gather(mid_feats[ranking], "grp", axis=0, tiled=True),
            lax.all_gather(high_feats[ranking], "grp", axis=0, tiled=True),
        ),
        weights,
    )
    ordered = partial_value[packed_index[source_rows]]
    summed = lax.psum_scatter(ordered, "tp", scatter_dimension=0, tiled=True)
    slab_rows = summed.shape[0]
    squares = lax.psum(jnp.sum(summed * summed, axis=1), "grp")
    inverse = lax.rsqrt(squares / D + EPSILON)
    normed = summed * inverse[:, None] * norm_gain[None, :]
    own_live = lax.dynamic_slice_in_dim(
        live_mask.reshape(total_tokens)[source_rows], lax.axis_index("tp") * slab_rows, slab_rows
    )
    return jnp.where(own_live[:, None] > 0, normed, jnp.zeros_like(normed)).astype(jnp.bfloat16)


def solution(mesh):
    in_specs = (
        P("grp", "tp"),
        P("grp", "tp"),
        P("grp", "tp"),
        P("tp", "grp"),
        P("tp", "grp"),
        P("tp", "grp"),
        P("grp"),
        P(),
        P(),
    )
    out_specs = P("tp", "grp")
    return jax.shard_map(
        per_device, mesh=mesh, in_specs=in_specs, out_specs=out_specs, check_vma=False
    )
```

profile of v0, /device:TPU:0, one launch (start us, length us, event | category | flops | bytes accessed | tf_op | source)
XLA Modules:
  0.0 187.8 jit_solution(15039944350763568591)
XLA Ops:
  6.5 0.0 copy-start
  6.5 0.0 all-gather.7.cloned.1.call-start
  6.5 0.8 le.52
  7.3 0.1 le.53
  7.4 0.1 le.54
  7.5 0.1 le.50
  7.6 2.0 %sort.17 = (s32[48]{0:T(128)}, s32[48]{0:T(128)S(1)}) sort(s32[48]{0:T(128)S(1)} %subtract_bitcast_fusion, s32[48]{0:T(128)S(1)} %iota.15), dimensions={0}, to_apply=%region_0.0 | sort | flops 288 | bytes 768 | tf_op jit(solution)/shard_map/jit(argsort)/sort | solution.py:38
  9.7 0.0 copy-start.3
  9.7 1.4 gather_fusion.1
  11.1 0.0 all-gather.7.cloned.1.call-update
  11.1 0.0 copy-start.6
  11.1 0.0 all-gather.9.cloned.1.call-start
  11.2 0.0 copy-done.2
  11.2 1.4 gather_fusion.2
  12.6 0.0 all-gather.9.cloned.1.call-update
  12.6 0.0 all-gather.11.cloned.1.call-start
  12.7 1.4 gather_fusion.3
  14.1 0.0 all-gather.11.cloned.1.call-update
  14.2 0.0 reduce-scatter.2.cloned.1.call-start
  14.2 0.2 reduce_window_sum.13
  14.4 0.1 le.57
  14.5 0.1 reduce_window_sum.14
  14.6 0.1 le.56
  14.7 0.0 copy-done.6
  14.7 0.1 add.94
  14.8 0.1 add.95
  14.9 0.1 iota_add_fusion
  15.0 0.1 add.87
  15.2 2.8 %gather_fusion.4 = s32[384]{0:T(512)S(1)} fusion(s32[384]{0:T(512)S(1)} %subtract_add_fusion, s32[1024]{0:T(1024)S(1)} %pad_clamp_fusion.2), kind=kCustom, calls=%fused_computation.4 | custom fusion | bytes 4608 | tf_op jit(solution)/shard_map/gather | solution.py:47
  18.0 25.2 %all-gather.7.cloned.1.call-done = bf16[256,4096]{1,0:T(8,128)(2,1)} async-done(((bf16[32,4096]{1,0:T(8,128)(2,1)}), bf16[256,4096]{1,0:T(8,128)(2,1)}) %all-gather.7.cloned.1.call-update) | async-done | bytes 2097168 | tf_op jit(solution)/shard_map/all_gather | solution.py:41
  43.2 8.7 %fusion.3 = f32[256,2048]{1,0:T(8,128)S(1)} fusion(bf16[256,4096]{1,0:T(8,128)(2,1)} %all-gather.7.cloned.1.call-done, bf16[4096,2048]{1,0:T(8,128)(2,1)} %param.12), kind=kOutput, calls=%fused_computation.28 | convolution fusion | flops 4294967296 | bytes 20971520 | tf_op jit(solution)/shard_map/dot_general | solution.py:15
  51.9 21.5 %all-gather.9.cloned.1.call-done = bf16[256,4096]{1,0:T(8,128)(2,1)} async-done(((bf16[32,4096]{1,0:T(8,128)(2,1)}), bf16[256,4096]{1,0:T(8,128)(2,1)}) %all-gather.9.cloned.1.call-update) | async-done | bytes 2097168 | tf_op jit(solution)/shard_map/all_gather | solution.py:42
  73.3 12.3 %convolution_add_fusion.1 = f32[256,2048]{1,0:T(8,128)} fusion(f32[256,2048]{1,0:T(8,128)S(1)} %fusion.3, bf16[256,4096]{1,0:T(8,128)(2,1)} %all-gather.9.cloned.1.call-done, bf16[4096,2048]{1,0:T(8,128)(2,1)} %param.13), kind=kOutput, calls=%fused_computation.7 | convolution fusion | flops 4295491584 | bytes 23068672 | tf_op jit(solution)/shard_map/dot_general | solution.py:16
  85.6 17.9 %all-gather.11.cloned.1.call-done = bf16[256,4096]{1,0:T(8,128)(2,1)} async-done(((bf16[32,4096]{1,0:T(8,128)(2,1)}), bf16[256,4096]{1,0:T(8,128)(2,1)}) %all-gather.11.cloned.1.call-update) | async-done | bytes 2097168 | tf_op jit(solution)/shard_map/all_gather | solution.py:43
  103.5 11.5 %convolution_add_fusion = f32[256,2048]{1,0:T(8,128)S(1)} fusion(f32[256,2048]{1,0:T(8,128)} %convolution_add_fusion.1, bf16[256,4096]{1,0:T(8,128)(2,1)} %all-gather.11.cloned.1.call-done, bf16[4096,2048]{1,0:T(8,128)(2,1)} %param.14), kind=kOutput, calls=%fused_computation.6 | convolution fusion | flops 4295491584 | bytes 23068672 | tf_op jit(solution)/shard_map/dot_general | solution.py:17
  115.0 3.3 %gather_fusion.5 = f32[384,2048]{1,0:T(8,128)} fusion(f32[256,2048]{1,0:T(8,128)S(1)} %convolution_add_fusion, s32[1024]{0:T(1024)S(1)} %pad_clamp_fusion), kind=kCustom, calls=%fused_computation.5 | custom fusion | bytes 6292992 | tf_op jit(solution)/shard_map/gather | solution.py:47
  118.3 0.0 reduce-scatter.2.cloned.1.call-update
  118.3 0.0 copy-start.4
  118.3 0.0 copy-start.1
  118.3 0.6 copy-done.5
  118.9 0.1 fusion
  119.0 0.1 reshape.72
  119.1 2.8 %gather_fusion = s32[384]{0:T(512)S(1)} fusion(s32[384]{0:T(512)S(1)} %reshape.72, s32[1024]{0:T(1024)S(1)} %pad_clamp_fusion.2), kind=kCustom, calls=%fused_computation | custom fusion | bytes 4608 | tf_op jit(solution)/shard_map/gather | solution.py:54
  121.9 0.1 dynamic-slice_compare_fusion
  122.0 39.7 %reduce-scatter.2.cloned.1.call-done = f32[96,2048]{1,0:T(8,128)} async-done(((f32[384,2048]{1,0:T(8,128)}), f32[96,2048]{1,0:T(8,128)}) %reduce-scatter.2.cloned.1.call-update) | async-done | bytes 786448 | tf_op jit(solution)/shard_map/reduce_scatter | solution.py:48
  161.8 1.3 multiply_reduce_fusion
  163.0 16.2 %psum.7 = f32[96]{0:T(128)S(1)} all-reduce(f32[96]{0:T(128)S(1)} %multiply_reduce_fusion), channel_id=1, replica_groups=mesh['tp'=4,'grp'=8] {'grp'}, use_global_device_ids=true, to_apply=%region_4.5 | all-reduce | flops 96 | bytes 768 | tf_op jit(solution)/shard_map/psum | solution.py:50
  179.2 2.0 %select_convert_fusion = bf16[96,2048]{1,0:T(8,128)(2,1)} fusion(f32[96,2048]{1,0:T(8,128)} %reduce-scatter.2.cloned.1.call-done, f32[2048]{0:T(1024)S(1)} %copy-done.4, f32[96]{0:T(128)S(1)} %add_rsqrt_fusion, pred[96]{0:T(512)(128)(4,1)S(1)} %dynamic-slice_compare_fusion), kind=kLoop, calls=%fused_computation.8 | loop fusion | flops 786432 | bytes 1188320 | tf_op jit(solution)/shard_map/convert_element_type | solution.py:56
  (21 shorter events, 0.1 us)
Async XLA Ops:
  6.5 3.1 %copy-start = (bf16[48,4096]{1,0:T(8,128)(2,1)S(1)}, bf16[48,4096]{1,0:T(8,128)(2,1)}, u32[]{:S(2)}) copy-start(bf16[48,4096]{1,0:T(8,128)(2,1)} %param.9) | copy-start | bytes 1179652
  6.5 4.7 %copy-start.2 = (bf16[48,4096]{1,0:T(8,128)(2,1)S(1)}, bf16[48,4096]{1,0:T(8,128)(2,1)}, u32[]{:S(2)}) copy-start(bf16[48,4096]{1,0:T(8,128)(2,1)} %param.10) | copy-start | bytes 1179652
  6.5 36.6 %all-gather.7.cloned.1.call-start = ((), (), s32[]{:S(2)}) async-start(), calls=%async_computation.2 | async-start | bytes 2359296 | tf_op jit(solution)/shard_map/all_gather | solution.py:41
  9.7 3.0 %copy-start.3 = (bf16[48,4096]{1,0:T(8,128)(2,1)S(1)}, bf16[48,4096]{1,0:T(8,128)(2,1)}, u32[]{:S(2)}) copy-start(bf16[48,4096]{1,0:T(8,128)(2,1)} %param.11) | copy-start | bytes 1179652
  11.1 3.6 %copy-start.6 = (s32[64]{0:T(128)S(1)}, s32[64]{0:T(128)}, u32[]{:S(2)}) copy-start(s32[64]{0:T(128)} %param.17) | copy-start | bytes 772
  11.1 62.2 %all-gather.9.cloned.1.call-start = ((), (), s32[]{:S(2)}) async-start(), calls=%async_computation.3 | async-start | bytes 2359296 | tf_op jit(solution)/shard_map/all_gather | solution.py:42
  12.6 90.9 %all-gather.11.cloned.1.call-start = ((), (), s32[]{:S(2)}) async-start(), calls=%async_computation.4 | async-start | bytes 2359296 | tf_op jit(solution)/shard_map/all_gather | solution.py:43
  14.2 147.6 %reduce-scatter.2.cloned.1.call-start = ((), (), s32[]{:S(2)}) async-start(), calls=%async_computation.1 | async-start | bytes 3932160 | tf_op jit(solution)/shard_map/reduce_scatter | solution.py:48
  118.3 0.7 copy-start.5
  118.3 60.9 %copy-start.4 = (f32[2048]{0:T(1024)S(1)}, f32[2048]{0:T(1024)}, u32[]{:S(2)}) copy-start(f32[2048]{0:T(1024)} %param.15) | copy-start | bytes 24580
  118.3 63.0 %copy-start.1 = (bf16[48,4096]{1,0:T(8,128)(2,1)S(1)}, bf16[48,4096]{1,0:T(8,128)(2,1)}, u32[]{:S(2)}) copy-start(bf16[48,4096]{1,0:T(8,128)(2,1)} %param.9) | copy-start | bytes 1179652
Sparse Core Ops, SparseCore 0:
  11.3 31.8 all-gather.6
  44.8 28.5 all-gather.8
  75.0 28.5 all-gather.10
  118.4 43.3 reduce-scatter.1
where the time goes:
time: 188 us
  waiting for transfers between devices  104 us (55%)
  matrix products  32.4 us (17%)
  blocking collectives  16.2 us (9%)
  local copies, waits for them, and re-layouts  15.5 us (8%)
  between operations  13.3 us (7%)
  other arithmetic  5.9 us (3%)
    reduce_scatter x1, waiting for transfers between devices, per_device(): summed = lax.psum_scatter(ordered, 'tp', scatter_dimension=0, tiled=True)  39.7 us
    all_gather x1, waiting for transfers between devices, per_device(): lax.all_gather(low_feats[ranking], 'grp', axis=0, tiled=True)  25.2 us
    all_gather x1, waiting for transfers between devices, per_device(): lax.all_gather(mid_feats[ranking], 'grp', axis=0, tiled=True)  21.5 us
    all_gather x1, waiting for transfers between devices, per_device(): lax.all_gather(high_feats[ranking], 'grp', axis=0, tiled=True)  17.9 us
    psum x1, blocking collectives, per_device(): squares = lax.psum(jnp.sum(summed * summed, axis=1), 'grp')  16.2 us
    dot_general x1, matrix products, project(): jnp.dot(features[1], weights[1], preferred_element_type=jnp.float32)  12.3 us
    dot_general x1, matrix products, project(): jnp.dot(features[2], weights[2], preferred_element_type=jnp.float32)  11.5 us
    dot_general x1, matrix products, project(): total = jnp.dot(features[0], weights[0], preferred_element_type=jnp.float32)  8.71 us
  transfers between devices with their start and end apart: 4, of which 4 were waited for; matrix products, arithmetic and copies ran while one was open for 16% of the time, Pallas kernels for 0%

commit v1 on v0

v1 whole, which is shorter than its diff:
```python
import functools

import jax
import jax.numpy as jnp
from jax import lax
from jax.experimental import pallas as pl
from jax.experimental.pallas import tpu as pltpu
from jax.sharding import PartitionSpec as P

ROWS_G = 8
POS = 6
CAPACITY = 4 * ROWS_G
BATCHES = 2
SLOTS = CAPACITY // BATCHES
LAYERS = 3
STEPS = BATCHES * LAYERS
AHEAD = 2
TILE = 256
EPSILON = 1e-05


def kernel(
    groups, owners,
    low_ref, mid_ref, high_ref, w_low, w_mid, w_high, gain_ref, pack_ref, pick_ref,
    out_ref,
    weights, blocks, sums, parts, squares, rows_out,
    w_sem, send_sem, recv_sem, part_send, part_recv, sq_send, sq_recv, row_send, row_recv,
):
    me = lax.axis_index("grp")
    own = lax.axis_index("tp")
    chip, core = me // 2, me % 2
    chips = groups // 2
    sibling = chip * 2 + 1 - core
    columns = sums.shape[2]
    share = rows_out.shape[2]
    width = groups * columns

    loads = [
        pltpu.make_async_copy(w, weights.at[i], w_sem.at[i])
        for i, w in enumerate((w_low, w_mid, w_high))
    ]
    for load in loads:
        load.start()

    barrier = pltpu.get_barrier_semaphore()
    for d in range(1, groups):
        pl.semaphore_signal(
            barrier, inc=1, device_id={"grp": lax.rem(me + d, groups)},
            device_id_type=pl.DeviceIdType.MESH,
        )
    for d in range(1, owners):
        pl.semaphore_signal(
            barrier, inc=1, device_id={"tp": lax.rem(own + d, owners)},
            device_id_type=pl.DeviceIdType.MESH,
        )

    def rows_of(group):
        return pl.ds(pl.multiple_of(group * SLOTS, SLOTS), SLOTS)

    for i, feats in enumerate((low_ref, mid_ref, high_ref)):
        packed = jnp.dot(
            pack_ref[...], feats[...], preferred_element_type=jnp.float32
        ).astype(jnp.bfloat16)
        for b in range(BATCHES):
            blocks[b * LAYERS + i, rows_of(me), :] = packed[b * SLOTS : (b + 1) * SLOTS]

    pl.semaphore_wait(barrier, groups + owners - 2)

    def block_copy(way, step, group):
        target = (chip * 2 + 2 + core, chip * 2 - 2 + core, sibling)[way]
        return pltpu.make_async_remote_copy(
            src_ref=blocks.at[step, rows_of(group), :],
            dst_ref=blocks.at[step, rows_of(group), :],
            send_sem=send_sem.at[way, step, group // 2],
            recv_sem=recv_sem.at[step, group],
            device_id={"grp": target},
            device_id_type=pl.DeviceIdType.MESH,
        )

    def send_own(step):
        @pl.when(chip < chips - 1)
        def _():
            block_copy(0, step, me).start()

        @pl.when(chip > 0)
        def _():
            block_copy(1, step, me).start()

        block_copy(2, step, me).start()

    def relay(step):
        for d in range(1, chips):
            @pl.when(chip - d >= 0)
            def _():
                group = me - 2 * d
                block_copy(0, step, group).wait_recv()

                @pl.when(chip < chips - 1)
                def _():
                    block_copy(0, step, group).start()

                block_copy(2, step, group).start()

            @pl.when(chip + d <= chips - 1)
            def _():
                group = me + 2 * d
                block_copy(1, step, group).wait_recv()

                @pl.when(chip > 0)
                def _():
                    block_copy(1, step, group).start()

                block_copy(2, step, group).start()
        for q in range(chips):
            block_copy(2, step, q * 2 + 1 - core).wait_recv()

    def multiply(step):
        b, layer = step // LAYERS, step % LAYERS

        @pl.loop(0, columns // TILE)
        def _(j):
            cols = pl.ds(pl.multiple_of(j * TILE, TILE), TILE)
            product = jnp.dot(
                blocks[step], weights[layer, :, cols], preferred_element_type=jnp.float32
            )
            if layer == 0:
                sums[b, :, cols] = product
            else:
                sums[b, :, cols] += product

    def share_of(owner):
        return pl.ds(pl.multiple_of(owner * share, share), share)

    def part_copy(b, d):
        target = lax.rem(own + d, owners)
        return pltpu.make_async_remote_copy(
            src_ref=sums.at[b, share_of(target), :],
            dst_ref=parts.at[b, d - 1],
            send_sem=part_send.at[b, d - 1],
            recv_sem=part_recv.at[b, d - 1],
            device_id={"tp": target},
            device_id_type=pl.DeviceIdType.MESH,
        )

    def square_copy(b, d):
        return pltpu.make_async_remote_copy(
            src_ref=squares.at[b, 0],
            dst_ref=squares.at[b, d],
            send_sem=sq_send.at[b, d - 1],
            recv_sem=sq_recv.at[b, d - 1],
            device_id={"grp": lax.rem(me + d, groups)},
            device_id_type=pl.DeviceIdType.MESH,
        )

    def row_copy(b, d):
        return pltpu.make_async_remote_copy(
            src_ref=rows_out.at[b, own],
            dst_ref=rows_out.at[b, own],
            send_sem=row_send.at[b, d - 1],
            recv_sem=row_recv.at[b, d - 1],
            device_id={"tp": lax.rem(own + d, owners)},
            device_id_type=pl.DeviceIdType.MESH,
        )

    diagonal = lax.broadcasted_iota(jnp.int32, (share, 128), 0) == lax.broadcasted_iota(
        jnp.int32, (share, 128), 1
    )

    def spread(b):
        for d in range(1, owners):
            part_copy(b, d).start()

    def reduce(b):
        total = sums[b, share_of(own), :]
        for d in range(1, owners):
            part_copy(b, d).wait_recv()
            total = total + parts[b, d - 1]
        parts[b, owners - 1] = total
        square = jnp.sum(total * total, axis=1, keepdims=True)
        lanes = jnp.sum(jnp.where(diagonal, square, 0.0), axis=0, keepdims=True)
        squares[b, 0] = jnp.broadcast_to(lanes, (8, 128))
        for d in range(1, groups):
            square_copy(b, d).start()

    def finish(b):
        for d in range(1, groups):
            square_copy(b, d).wait_recv()
        lanes = squares[b, 0]
        for d in range(1, groups):
            lanes = lanes + squares[b, d]
        square = jnp.sum(jnp.where(diagonal, lanes[0:1], 0.0), axis=1, keepdims=True)
        inverse = lax.rsqrt(square / width + EPSILON)
        rows_out[b, own] = (parts[b, owners - 1] * inverse * gain_ref[...]).astype(jnp.bfloat16)
        for d in range(1, owners):
            row_copy(b, d).start()

    for step in range(AHEAD):
        send_own(step)
    for step in range(STEPS):
        if step + AHEAD < STEPS:
            send_own(step + AHEAD)
        relay(step)
        if step < LAYERS:
            loads[step].wait()
        multiply(step)
        if step % LAYERS == LAYERS - 1:
            spread(step // LAYERS)
        if step >= LAYERS and step % LAYERS == 0:
            reduce(step // LAYERS - 1)
        if step >= LAYERS and step % LAYERS == 1:
            finish(step // LAYERS - 1)
    reduce(BATCHES - 1)
    finish(BATCHES - 1)
    for b in range(BATCHES):
        for d in range(1, owners):
            row_copy(b, d).wait_recv()

    everything = rows_out[...].reshape(BATCHES * owners * share, columns)
    out_ref[...] = jnp.dot(
        pick_ref[...], everything, preferred_element_type=jnp.float32
    ).astype(jnp.bfloat16)

    for step in range(STEPS):
        for q in range(chips):
            group = q * 2 + core

            @pl.when((chip < chips - 1) & (q <= chip))
            def _():
                block_copy(0, step, group).wait_send()

            @pl.when((chip > 0) & (q >= chip))
            def _():
                block_copy(1, step, group).wait_send()

            block_copy(2, step, group).wait_send()
    for b in range(BATCHES):
        for d in range(1, owners):
            part_copy(b, d).wait_send()
            row_copy(b, d).wait_send()
        for d in range(1, groups):
            square_copy(b, d).wait_send()


def per_device(
    groups, owners,
    low_feats, mid_feats, high_feats, w_low, w_mid, w_high, norm_gain, accepted, assignment,
):
    tokens, depth = low_feats.shape
    columns = w_low.shape[1]
    rows = accepted.shape[0]
    batch_rows = groups * SLOTS
    share = batch_rows // owners
    slab = rows * POS // owners

    row = jnp.arange(rows, dtype=jnp.int32)
    position = jnp.arange(POS, dtype=jnp.int32)
    before = jnp.where(row % 2 == 1, jnp.roll(accepted, 1) + 1, 0)
    local = row % ROWS_G
    first_slot = (local // 2) * (2 * CAPACITY // ROWS_G) + before
    slot = first_slot[:, None] + position[None, :]
    live = position[None, :] <= accepted[:, None]
    slot = jnp.where(live, slot, -1)
    me = lax.axis_index("grp")
    own_slot = lax.dynamic_slice_in_dim(slot, me * ROWS_G, ROWS_G).reshape(tokens)
    pack = (jnp.arange(CAPACITY, dtype=jnp.int32)[:, None] == own_slot[None, :]).astype(
        jnp.bfloat16
    )
    place = jnp.where(
        live,
        (slot // SLOTS) * batch_rows + (row // ROWS_G)[:, None] * SLOTS + slot % SLOTS,
        -1,
    )
    own_assignment = lax.dynamic_slice_in_dim(
        assignment, lax.axis_index("tp") * (rows // owners), rows // owners
    )
    taken = own_assignment[:, None] == row[None, :]
    own_place = jnp.sum(jnp.where(taken[:, :, None], place[None], 0), axis=1).reshape(slab)
    pick = (
        own_place[:, None] == jnp.arange(BATCHES * batch_rows, dtype=jnp.int32)[None, :]
    ).astype(jnp.bfloat16)

    vmem = pl.BlockSpec(memory_space=pltpu.VMEM)
    hbm = pl.BlockSpec(memory_space=pl.ANY)
    dma = pltpu.SemaphoreType.DMA
    return pl.pallas_call(
        functools.partial(kernel, groups, owners),
        out_shape=jax.ShapeDtypeStruct((slab, columns), jnp.bfloat16),
        in_specs=[vmem] * 3 + [hbm] * 3 + [vmem] * 3,
        out_specs=vmem,
        scratch_shapes=[
            pltpu.VMEM((LAYERS, depth, columns), jnp.bfloat16),
            pltpu.VMEM((STEPS, batch_rows, depth), jnp.bfloat16),
            pltpu.VMEM((BATCHES, batch_rows, columns), jnp.float32),
            pltpu.VMEM((BATCHES, owners, share, columns), jnp.float32),
            pltpu.VMEM((BATCHES, groups, 8, 128), jnp.float32),
            pltpu.VMEM((BATCHES, owners, share, columns), jnp.bfloat16),
            dma((LAYERS,)),
            dma((3, STEPS, groups // 2)),
            dma((STEPS, groups)),
            dma((BATCHES, owners - 1)),
            dma((BATCHES, owners - 1)),
            dma((BATCHES, groups - 1)),
            dma((BATCHES, groups - 1)),
            dma((BATCHES, owners - 1)),
            dma((BATCHES, owners - 1)),
        ],
        compiler_params=pltpu.CompilerParams(
            collective_id=0, has_side_effects=True, vmem_limit_bytes=67043328
        ),
    )(low_feats, mid_feats, high_feats, w_low, w_mid, w_high, norm_gain[None, :], pack, pick)


def solution(mesh):
    in_specs = (
        P("grp", "tp"),
        P("grp", "tp"),
        P("grp", "tp"),
        P("tp", "grp"),
        P("tp", "grp"),
        P("tp", "grp"),
        P("grp"),
        P(),
        P(),
    )
    return jax.shard_map(
        functools.partial(per_device, mesh.shape["grp"], mesh.shape["tp"]),
        mesh=mesh,
        in_specs=in_specs,
        out_specs=P("tp", "grp"),
        check_vma=False,
    )
```

time: 188 us -> 124 us (0.66)
  Pallas kernels: 0 us -> 116 us
  waiting for transfers between devices: 104 us -> 0 us
  matrix products: 32.4 us -> 0 us
  blocking collectives: 16.2 us -> 0 us
  between operations: 13.3 us -> 0.04 us
  local copies, waits for them, and re-layouts: 15.5 us -> 4.06 us
  other arithmetic: 5.9 us -> 3.71 us
    pallas_call x0 -> x1, Pallas kernels: none -> 116 us  [per_device(): pl.pallas_call(functools.partial(kernel, groups, owners), out_shape=jax.S...]
    all_gather x3 -> x0, waiting for transfers between devices: 64.5 us -> none  [the longest x1 25.2 us: per_device(): lax.all_gather(low_feats[ranking], 'grp', axis=0, tiled=True)]
    reduce_scatter x1 -> x0, waiting for transfers between devices: 39.7 us -> none  [per_device(): summed = lax.psum_scatter(ordered, 'tp', scatter_dimension=0, tiled=True)]
    dot_general x3 -> x0, matrix products: 32.4 us -> none  [the longest x1 12.3 us: project(): jnp.dot(features[1], weights[1], preferred_element_type=jnp.float32)]
    psum x1 -> x0, blocking collectives: 16.2 us -> none  [per_device(): squares = lax.psum(jnp.sum(summed * summed, axis=1), 'grp')]
    gather x6 -> x0, local copies, waits for them, and re-layouts: 13.1 us -> none  [the longest x2 6.06 us: per_device(): ordered = partial_value[packed_index[source_rows]]]
    sort x1 -> x0, other arithmetic: 2.04 us -> none  [per_device(): ranking = jnp.argsort(1 - own_group, stable=True)[:capacity]]
  transfers between devices with their start and end apart: 4 -> 0, of which waited for: 4 -> 0; matrix products, arithmetic and copies ran while one was open for 16% -> 0% of each run, Pallas kernels for 0% -> 0%
where the time goes in v1:
time: 124 us
  Pallas kernels  116 us (94%)
  local copies, waits for them, and re-layouts  4.06 us (3%)
  other arithmetic  3.71 us (3%)
    pallas_call x1, Pallas kernels, per_device(): pl.pallas_call(functools.partial(kernel, groups, owners), out_shape=jax.S...  116 us

profile of v1, /device:TPU:0, one launch (start us, length us, event | category | flops | bytes accessed | tf_op | source)
XLA Modules:
  0.0 124.2 jit_solution(3796420061593012934)
XLA Ops:
  0.0 1.2 slice.8
  1.2 0.7 dynamic_slice.7
  2.0 1.4 %fusion.10 = (s32[64]{0:T(128)S(1)}, s32[64]{0:T(128)S(1)}) fusion(s32[63]{0:T(128)} %bitcast.3, s32[1]{0:T(128)} %slice.8), kind=kLoop, calls=%fused_computation.32 | loop fusion | flops 2560 | bytes 768 | tf_op jit(solution)/shard_map/add | solution.py:259
  3.3 0.1 iota_compare_fusion.3
  3.4 0.8 fusion.4
  4.2 0.1 copy.10
  4.3 0.2 select_reduce_fusion
  4.5 0.1 eq.61
  4.5 0.1 copy.11
  4.6 0.1 eq.67
  4.7 0.6 fusion.9.pack_ref
  5.3 0.7 fusion.pick_ref
  6.0 116.4 %shard_map.91 = bf16[96,2048]{1,0:T(8,128)(2,1)} custom-call(bf16[48,4096]{1,0:T(8,128)(2,1)} %low_ref.1, bf16[48,4096]{1,0:T(8,128)(2,1)} %mid_ref.1, bf16[48,4096]{1,0:T(8,128)(2,1)} %high_ref.1, bf16[4096,2048]{1,0:T(8,128)(2,1)} %w_low.1, bf16[4096,2048]{1,0:T(8,128)(2,1)} %w_mid.1, bf16[4096,2048]{1,0:T(8,128)(2,1)} %w_high.1, f32[1,2048]{1,0:T(1,128)} %bitcast.2, ...), custom_call_target="tpu_custom_call" | custom-call | tf_op jit(solution)/shard_map/pallas_call | solution.py:285
  122.4 1.8 %copy.13 = bf16[96,2048]{1,0:T(8,128)(2,1)} copy(bf16[96,2048]{1,0:T(8,128)(2,1)} %shard_map.91) | data formatting | bytes 786432
  (1 shorter events, 0.0 us)

commit v2 on v1

v2 whole, which is shorter than its diff:
```python
import functools

import jax
import jax.numpy as jnp
from jax import lax
from jax.experimental import pallas as pl
from jax.experimental.pallas import tpu as pltpu
from jax.sharding import PartitionSpec as P

ROWS_G = 8
POS = 6
CAPACITY = 4 * ROWS_G
BATCHES = 2
SLOTS = CAPACITY // BATCHES
LAYERS = 3
STEPS = BATCHES * LAYERS
AHEAD = 2
TILE = 256
EPSILON = 1e-05


def kernel(
    groups, owners,
    low_ref, mid_ref, high_ref, w_low, w_mid, w_high, gain_ref, accepted_ref, assignment_ref,
    out_ref,
    feats, weights, blocks, sums, parts, squares, rows_out, pick,
    f_sem, w_sem, send_sem, recv_sem, part_send, part_recv, sq_send, sq_recv, row_send, row_recv,
):
    me = lax.axis_index("grp")
    own = lax.axis_index("tp")
    chip, core = me // 2, me % 2
    chips = groups // 2
    sibling = chip * 2 + 1 - core
    columns = sums.shape[2]
    share = rows_out.shape[2]
    width = groups * columns
    tiles = columns // TILE
    tokens = feats.shape[1]
    slab = out_ref.shape[0]
    pair_slots = 2 * CAPACITY // ROWS_G

    reads = [
        pltpu.make_async_copy(f, feats.at[i], f_sem.at[i])
        for i, f in enumerate((low_ref, mid_ref, high_ref))
    ]
    for read in reads:
        read.start()
    loads = [
        pltpu.make_async_copy(w, weights.at[i], w_sem.at[i])
        for i, w in enumerate((w_low, w_mid, w_high))
    ]

    barrier = pltpu.get_barrier_semaphore()
    for d in range(1, groups):
        pl.semaphore_signal(
            barrier, inc=1, device_id={"grp": lax.rem(me + d, groups)},
            device_id_type=pl.DeviceIdType.MESH,
        )
    for d in range(1, owners):
        pl.semaphore_signal(
            barrier, inc=1, device_id={"tp": lax.rem(own + d, owners)},
            device_id_type=pl.DeviceIdType.MESH,
        )

    def rows_of(group):
        return pl.ds(pl.multiple_of(group * SLOTS, SLOTS), SLOTS)

    slot = lax.broadcasted_iota(jnp.int32, (CAPACITY, tokens), 0)
    token = lax.broadcasted_iota(jnp.int32, (CAPACITY, tokens), 1)
    packing = jnp.zeros((CAPACITY, tokens), jnp.float32)
    for k in range(ROWS_G):
        count = accepted_ref[me * ROWS_G + k] + 1
        start = (k // 2) * pair_slots
        if k % 2 == 1:
            start = start + accepted_ref[me * ROWS_G + k - 1] + 1
        position = token - k * POS
        hit = (position >= 0) & (position < count) & (slot == start + position)
        packing = jnp.where(hit, 1.0, packing)
    packing = packing.astype(jnp.bfloat16)

    def pack(layer):
        reads[layer].wait()
        packed = jnp.dot(packing, feats[layer], preferred_element_type=jnp.float32)
        for b in range(BATCHES):
            blocks[b * LAYERS + layer, rows_of(me), :] = packed[
                b * SLOTS : (b + 1) * SLOTS
            ].astype(jnp.bfloat16)

    pack(0)
    pl.semaphore_wait(barrier, groups + owners - 2)

    def block_copy(way, step, group):
        target = (chip * 2 + 2 + core, chip * 2 - 2 + core, sibling)[way]
        return pltpu.make_async_remote_copy(
            src_ref=blocks.at[step, rows_of(group), :],
            dst_ref=blocks.at[step, rows_of(group), :],
            send_sem=send_sem.at[way, step, group // 2],
            recv_sem=recv_sem.at[step, group],
            device_id={"grp": target},
            device_id_type=pl.DeviceIdType.MESH,
        )

    def send_own(step):
        @pl.when(chip < chips - 1)
        def _():
            block_copy(0, step, me).start()

        @pl.when(chip > 0)
        def _():
            block_copy(1, step, me).start()

        block_copy(2, step, me).start()

    def relay(step, d):
        @pl.when(chip - d >= 0)
        def _():
            group = me - 2 * d
            block_copy(0, step, group).wait_recv()

            @pl.when(chip < chips - 1)
            def _():
                block_copy(0, step, group).start()

            block_copy(2, step, group).start()

        @pl.when(chip + d <= chips - 1)
        def _():
            group = me + 2 * d
            block_copy(1, step, group).wait_recv()

            @pl.when(chip > 0)
            def _():
                block_copy(1, step, group).start()

            block_copy(2, step, group).start()

    def relays(step, first, last):
        @pl.loop(first, last)
        def _(d):
            relay(step, d)

    def arrive(step):
        for q in range(chips):
            block_copy(2, step, q * 2 + 1 - core).wait_recv()

    def multiply(step):
        b, layer = step // LAYERS, step % LAYERS

        @pl.loop(0, tiles)
        def _(j):
            cols = pl.ds(pl.multiple_of(j * TILE, TILE), TILE)
            product = jnp.dot(
                blocks[step], weights[layer, :, cols], preferred_element_type=jnp.float32
            )
            if layer == 0:
                sums[b, :, cols] = product
            else:
                sums[b, :, cols] += product
            if layer == LAYERS - 1:
                for d in range(1, owners):
                    part_copy(b, d, j).start()
            if step + 1 < STEPS:
                relays(
                    step + 1,
                    1 + (chips - 1) * j // tiles,
                    1 + (chips - 1) * (j + 1) // tiles,
                )
            if b > 0 and layer == 1:
                @pl.when(j == tiles // 2)
                def _():
                    reduce(b - 1)

    def share_of(owner):
        return pl.ds(pl.multiple_of(owner * share, share), share)

    def part_copy(b, d, j):
        cols = pl.ds(pl.multiple_of(j * TILE, TILE), TILE)
        target = lax.rem(own + d, owners)
        return pltpu.make_async_remote_copy(
            src_ref=sums.at[b, share_of(target), cols],
            dst_ref=parts.at[b, d - 1, :, cols],
            send_sem=part_send.at[b, d - 1, j],
            recv_sem=part_recv.at[b, d - 1, j],
            device_id={"tp": target},
            device_id_type=pl.DeviceIdType.MESH,
        )

    def square_copy(b, d):
        return pltpu.make_async_remote_copy(
            src_ref=squares.at[b, 0],
            dst_ref=squares.at[b, d],
            send_sem=sq_send.at[b, d - 1],
            recv_sem=sq_recv.at[b, d - 1],
            device_id={"grp": lax.rem(me + d, groups)},
            device_id_type=pl.DeviceIdType.MESH,
        )

    def row_copy(b, d):
        return pltpu.make_async_remote_copy(
            src_ref=rows_out.at[b, own],
            dst_ref=rows_out.at[b, own],
            send_sem=row_send.at[b, d - 1],
            recv_sem=row_recv.at[b, d - 1],
            device_id={"tp": lax.rem(own + d, owners)},
            device_id_type=pl.DeviceIdType.MESH,
        )

    diagonal = lax.broadcasted_iota(jnp.int32, (share, 128), 0) == lax.broadcasted_iota(
        jnp.int32, (share, 128), 1
    )

    def reduce(b):
        def body(j, square):
            cols = pl.ds(pl.multiple_of(j * TILE, TILE), TILE)
            total = sums[b, share_of(own), cols]
            for d in range(1, owners):
                part_copy(b, d, j).wait_recv()
                total = total + parts[b, d - 1, :, cols]
            parts[b, owners - 1, :, cols] = total
            return square + jnp.sum(total * total, axis=1, keepdims=True)

        square = lax.fori_loop(0, tiles, body, jnp.zeros((share, 1), jnp.float32))
        lanes = jnp.sum(jnp.where(diagonal, square, 0.0), axis=0, keepdims=True)
        squares[b, 0] = jnp.broadcast_to(lanes, (8, 128))
        for d in range(1, groups):
            square_copy(b, d).start()

    def finish(b):
        for d in range(1, groups):
            square_copy(b, d).wait_recv()
        lanes = squares[b, 0]
        for d in range(1, groups):
            lanes = lanes + squares[b, d]
        square = jnp.sum(jnp.where(diagonal, lanes[0:1], 0.0), axis=1, keepdims=True)
        inverse = lax.rsqrt(square / width + EPSILON)
        rows_out[b, own] = (parts[b, owners - 1] * inverse * gain_ref[...]).astype(jnp.bfloat16)
        for d in range(1, owners):
            row_copy(b, d).start()

    send_own(0)
    pack(1)
    send_own(1)
    for load in loads:
        load.start()
    pack(2)

    column = lax.broadcasted_iota(jnp.int32, pick.shape, 1)
    batch_rows = groups * SLOTS
    batch_bits, slot_bits = batch_rows.bit_length() - 1, SLOTS.bit_length() - 1
    group_of = lax.shift_right_logical(column & (batch_rows - 1), slot_bits)
    slot_of = lax.shift_right_logical(column, batch_bits) * SLOTS + (column & (SLOTS - 1))
    place = group_of * CAPACITY + slot_of
    line = lax.broadcasted_iota(jnp.int32, pick.shape, 0)
    picking = jnp.zeros(pick.shape, jnp.float32)
    for k in range(slab // POS):
        source = assignment_ref[own * (slab // POS) + k]
        count = accepted_ref[source] + 1
        local = source & (ROWS_G - 1)
        odd = local & 1
        before = (accepted_ref[jnp.maximum(source - 1, 0)] + 1) * odd
        start = (source - local) // ROWS_G * CAPACITY + (local - odd) // 2 * pair_slots + before
        position = line - k * POS
        hit = (position >= 0) & (position < count) & (place == start + position)
        picking = jnp.where(hit, 1.0, picking)
    pick[...] = picking.astype(jnp.bfloat16)

    relays(0, 1, chips)
    arrive(0)
    for step in range(STEPS):
        if step + AHEAD < STEPS:
            send_own(step + AHEAD)
        if step < LAYERS:
            loads[step].wait()
        multiply(step)
        if step + 1 < STEPS:
            arrive(step + 1)
        if step >= LAYERS and step % LAYERS == 1:
            finish(step // LAYERS - 1)
    reduce(BATCHES - 1)
    finish(BATCHES - 1)
    for b in range(BATCHES):
        for d in range(1, owners):
            row_copy(b, d).wait_recv()

    everything = rows_out[...].reshape(BATCHES * owners * share, columns)
    out_ref[...] = jnp.dot(
        pick[...], everything, preferred_element_type=jnp.float32
    ).astype(jnp.bfloat16)

    for step in range(STEPS):
        for q in range(chips):
            group = q * 2 + core

            @pl.when((chip < chips - 1) & (q <= chip))
            def _():
                block_copy(0, step, group).wait_send()

            @pl.when((chip > 0) & (q >= chip))
            def _():
                block_copy(1, step, group).wait_send()

            block_copy(2, step, group).wait_send()
    for b in range(BATCHES):
        for d in range(1, owners):
            @pl.loop(0, tiles)
            def _(j):
                part_copy(b, d, j).wait_send()

            row_copy(b, d).wait_send()
        for d in range(1, groups):
            square_copy(b, d).wait_send()


def per_device(
    groups, owners,
    low_feats, mid_feats, high_feats, w_low, w_mid, w_high, norm_gain, accepted, assignment,
):
    tokens, depth = low_feats.shape
    columns = w_low.shape[1]
    rows = accepted.shape[0]
    batch_rows = groups * SLOTS
    share = batch_rows // owners
    slab = rows * POS // owners

    vmem = pl.BlockSpec(memory_space=pltpu.VMEM)
    hbm = pl.BlockSpec(memory_space=pl.ANY)
    smem = pl.BlockSpec(memory_space=pltpu.SMEM)
    dma = pltpu.SemaphoreType.DMA
    return pl.pallas_call(
        functools.partial(kernel, groups, owners),
        out_shape=jax.ShapeDtypeStruct((slab, columns), jnp.bfloat16),
        in_specs=[hbm] * 6 + [vmem] + [smem] * 2,
        out_specs=vmem,
        scratch_shapes=[
            pltpu.VMEM((LAYERS, tokens, depth), jnp.bfloat16),
            pltpu.VMEM((LAYERS, depth, columns), jnp.bfloat16),
            pltpu.VMEM((STEPS, batch_rows, depth), jnp.bfloat16),
            pltpu.VMEM((BATCHES, batch_rows, columns), jnp.float32),
            pltpu.VMEM((BATCHES, owners, share, columns), jnp.float32),
            pltpu.VMEM((BATCHES, groups, 8, 128), jnp.float32),
            pltpu.VMEM((BATCHES, owners, share, columns), jnp.bfloat16),
            pltpu.VMEM((slab, BATCHES * batch_rows), jnp.bfloat16),
            dma((LAYERS,)),
            dma((LAYERS,)),
            dma((3, STEPS, groups // 2)),
            dma((STEPS, groups)),
            dma((BATCHES, owners - 1, columns // TILE)),
            dma((BATCHES, owners - 1, columns // TILE)),
            dma((BATCHES, groups - 1)),
            dma((BATCHES, groups - 1)),
            dma((BATCHES, owners - 1)),
            dma((BATCHES, owners - 1)),
        ],
        compiler_params=pltpu.CompilerParams(
            collective_id=0, has_side_effects=True, vmem_limit_bytes=67043328
        ),
    )(low_feats, mid_feats, high_feats, w_low, w_mid, w_high, norm_gain[None, :], accepted, assignment)


def solution(mesh):
    in_specs = (
        P("grp", "tp"),
        P("grp", "tp"),
        P("grp", "tp"),
        P("tp", "grp"),
        P("tp", "grp"),
        P("tp", "grp"),
        P("grp"),
        P(),
        P(),
    )
    return jax.shard_map(
        functools.partial(per_device, mesh.shape["grp"], mesh.shape["tp"]),
        mesh=mesh,
        in_specs=in_specs,
        out_specs=P("tp", "grp"),
        check_vma=False,
    )
```

time: 124 us -> 99.4 us (0.80)
  Pallas kernels: 116 us -> 97.4 us
  other arithmetic: 3.71 us -> 0 us
  local copies, waits for them, and re-layouts: 4.06 us -> 1.77 us
    pallas_call x1, Pallas kernels: 116 us -> 97.4 us  [per_device(): pl.pallas_call(functools.partial(kernel, groups, owners), out_shape=jax.S...]
    add x1 -> x0, other arithmetic: 1.38 us -> none  [per_device(): first_slot = local // 2 * (2 * CAPACITY // ROWS_G) + before]
    convert_element_type x2 -> x0, other arithmetic: 1.31 us -> none  [the longest x1 0.7 us: per_device(): pick = (own_place[:, None] == jnp.arange(BATCHES * batch_rows, dtype=jnp....]
where the time goes in v2:
time: 99.4 us; the launch traced here: 99.1 us
  Pallas kernels  97.4 us (98%)
  local copies, waits for them, and re-layouts  1.77 us (2%)
    pallas_call x1, Pallas kernels, per_device(): pl.pallas_call(functools.partial(kernel, groups, owners), out_shape=jax.S...  97.4 us

profile of v2, /device:TPU:0, one launch (start us, length us, event | category | flops | bytes accessed | tf_op | source)
XLA Modules:
  0.0 99.1 jit_solution(16729418336502606245)
XLA Ops:
  0.0 97.4 %shard_map.91 = bf16[96,2048]{1,0:T(8,128)(2,1)} custom-call(bf16[48,4096]{1,0:T(8,128)(2,1)} %low_ref.1, bf16[48,4096]{1,0:T(8,128)(2,1)} %mid_ref.1, bf16[48,4096]{1,0:T(8,128)(2,1)} %high_ref.1, bf16[4096,2048]{1,0:T(8,128)(2,1)} %w_low.1, bf16[4096,2048]{1,0:T(8,128)(2,1)} %w_mid.1, bf16[4096,2048]{1,0:T(8,128)(2,1)} %w_high.1, f32[1,2048]{1,0:T(1,128)} %bitcast.1, ...), custom_call_target="tpu_custom_call" | custom-call | tf_op jit(solution)/shard_map/pallas_call | solution.py:329
  97.4 1.8 %copy.11 = bf16[96,2048]{1,0:T(8,128)(2,1)} copy(bf16[96,2048]{1,0:T(8,128)(2,1)} %shard_map.91) | data formatting | bytes 786432

commit v3 on v2

--- a/solution.py
+++ b/solution.py
@@ -16,6 +16,7 @@
 STEPS = BATCHES * LAYERS
 AHEAD = 2
 TILE = 256
+PIECES = 1
 EPSILON = 1e-05
 
 
@@ -157,8 +158,11 @@
             else:
                 sums[b, :, cols] += product
             if layer == LAYERS - 1:
-                for d in range(1, owners):
-                    part_copy(b, d, j).start()
+                @pl.when(j % piece_tiles == piece_tiles - 1)
+                def _():
+                    for d in range(1, owners):
+                        part_copy(b, d, j // piece_tiles).start()
+
             if step + 1 < STEPS:
                 relays(
                     step + 1,
@@ -173,14 +177,17 @@
     def share_of(owner):
         return pl.ds(pl.multiple_of(owner * share, share), share)
 
-    def part_copy(b, d, j):
-        cols = pl.ds(pl.multiple_of(j * TILE, TILE), TILE)
+    piece = columns // PIECES
+    piece_tiles = tiles // PIECES
+
+    def part_copy(b, d, h):
+        cols = pl.ds(pl.multiple_of(h * piece, piece), piece)
         target = lax.rem(own + d, owners)
         return pltpu.make_async_remote_copy(
             src_ref=sums.at[b, share_of(target), cols],
             dst_ref=parts.at[b, d - 1, :, cols],
-            send_sem=part_send.at[b, d - 1, j],
-            recv_sem=part_recv.at[b, d - 1, j],
+            send_sem=part_send.at[b, d - 1, h],
+            recv_sem=part_recv.at[b, d - 1, h],
             device_id={"tp": target},
             device_id_type=pl.DeviceIdType.MESH,
         )
@@ -210,16 +217,16 @@
     )
 
     def reduce(b):
-        def body(j, square):
-            cols = pl.ds(pl.multiple_of(j * TILE, TILE), TILE)
+        def body(h, square):
+            cols = pl.ds(pl.multiple_of(h * piece, piece), piece)
             total = sums[b, share_of(own), cols]
             for d in range(1, owners):
-                part_copy(b, d, j).wait_recv()
+                part_copy(b, d, h).wait_recv()
                 total = total + parts[b, d - 1, :, cols]
             parts[b, owners - 1, :, cols] = total
             return square + jnp.sum(total * total, axis=1, keepdims=True)
 
-        square = lax.fori_loop(0, tiles, body, jnp.zeros((share, 1), jnp.float32))
+        square = lax.fori_loop(0, PIECES, body, jnp.zeros((share, 1), jnp.float32))
         lanes = jnp.sum(jnp.where(diagonal, square, 0.0), axis=0, keepdims=True)
         squares[b, 0] = jnp.broadcast_to(lanes, (8, 128))
         for d in range(1, groups):
@@ -274,7 +281,7 @@
         multiply(step)
         if step + 1 < STEPS:
             arrive(step + 1)
-        if step >= LAYERS and step % LAYERS == 1:
+        if step >= LAYERS and step % LAYERS == 2:
             finish(step // LAYERS - 1)
     reduce(BATCHES - 1)
     finish(BATCHES - 1)
@@ -302,10 +309,8 @@
             block_copy(2, step, group).wait_send()
     for b in range(BATCHES):
         for d in range(1, owners):
-            @pl.loop(0, tiles)
-            def _(j):
-                part_copy(b, d, j).wait_send()
-
+            for h in range(PIECES):
+                part_copy(b, d, h).wait_send()
             row_copy(b, d).wait_send()
         for d in range(1, groups):
             square_copy(b, d).wait_send()
@@ -344,8 +349,8 @@
             dma((LAYERS,)),
             dma((3, STEPS, groups // 2)),
             dma((STEPS, groups)),
-            dma((BATCHES, owners - 1, columns // TILE)),
-            dma((BATCHES, owners - 1, columns // TILE)),
+            dma((BATCHES, owners - 1, PIECES)),
+            dma((BATCHES, owners - 1, PIECES)),
             dma((BATCHES, groups - 1)),
             dma((BATCHES, groups - 1)),
             dma((BATCHES, owners - 1)),

time: 99.4 us -> 97.4 us (0.980)
  Pallas kernels: 97.4 us -> 95.4 us
    pallas_call x1, Pallas kernels: 97.4 us -> 95.4 us  [per_device(): pl.pallas_call(functools.partial(kernel, groups, owners), out_shape=jax.S...]
where the time goes in v3:
time: 97.4 us; the launch traced here: 97.2 us
  Pallas kernels  95.4 us (98%)
  local copies, waits for them, and re-layouts  1.77 us (2%)
    pallas_call x1, Pallas kernels, per_device(): pl.pallas_call(functools.partial(kernel, groups, owners), out_shape=jax.S...  95.4 us

profile of v3, /device:TPU:0, one launch (start us, length us, event | category | flops | bytes accessed | tf_op | source)
XLA Modules:
  0.0 97.2 jit_solution(12034198845193585272)
XLA Ops:
  0.0 95.4 %shard_map.91 = bf16[96,2048]{1,0:T(8,128)(2,1)} custom-call(bf16[48,4096]{1,0:T(8,128)(2,1)} %low_ref.1, bf16[48,4096]{1,0:T(8,128)(2,1)} %mid_ref.1, bf16[48,4096]{1,0:T(8,128)(2,1)} %high_ref.1, bf16[4096,2048]{1,0:T(8,128)(2,1)} %w_low.1, bf16[4096,2048]{1,0:T(8,128)(2,1)} %w_mid.1, bf16[4096,2048]{1,0:T(8,128)(2,1)} %w_high.1, f32[1,2048]{1,0:T(1,128)} %bitcast.1, ...), custom_call_target="tpu_custom_call" | custom-call | tf_op jit(solution)/shard_map/pallas_call | solution.py:334
  95.4 1.8 %copy.11 = bf16[96,2048]{1,0:T(8,128)(2,1)} copy(bf16[96,2048]{1,0:T(8,128)(2,1)} %shard_map.91) | data formatting | bytes 786432
